TPU v7x, 512 devices: a whole 4x8x8 slice. The times are simulated.
512 devices in a mesh: section: 16 (over z, y_hi), dp: 32 (over x, y_lo, core).
Axes of the slice: x: 4, y: 8 (y_hi: 2, y_lo: 4; y = y_hi * 4 + y_lo), z: 8, core: 2. Of those that a mesh axis runs over, the one named last changes fastest.
Arguments:
- tokens: bfloat16 [8192, 4096], P('dp'), may hold values from -48 to 48
- orig_weight: bfloat16 [16384, 4096], P(('section', 'dp')), may hold values from -6 to 6
- keep_flags: int32 [64], replicated, may hold values from 0 to 1, as said below
Outputs:
- corrected: bfloat16 [16384, 4096], P(('section', 'dp'))
Inputs may be any that keep to these rules, and one draw needn't show every extreme that they name: `keep_flags`: exactly 12 of the 64 flags are 1.
All inputs are finite; a program needn't handle non-finite values.
Results may differ from a plain program's by a relative error of at most 0.003.
Values may be sent and summed in bfloat16 or wider, within the bound.
A program may use at most 64 MiB of HBM per device.

v0:
```python
import jax
import jax.numpy as jnp
from jax import lax
from jax.sharding import PartitionSpec as P

KEEP_BLK = 12


def on_device(tokens, orig_weight, keep_flags):
    highest = lax.Precision.HIGHEST
    feature_count = tokens.shape[1]
    blocks = jnp.nonzero(keep_flags, size=KEEP_BLK)[0].astype(jnp.int32)
    kept_index = (
        (blocks[:, None] * 64 + jnp.arange(64, dtype=jnp.int32)[None, :])
        .reshape(-1)
        .astype(jnp.int32)
    )
    kept_tokens = jnp.take(tokens, kept_index, axis=1)
    kept_count = kept_tokens.shape[1]
    section_count = lax.axis_size("section")
    rows_each = tokens.shape[0] // section_count
    first_row = lax.axis_index("section") * rows_each
    part_kept = lax.dynamic_slice_in_dim(kept_tokens, first_row, rows_each, 0)
    part_tokens = lax.dynamic_slice_in_dim(tokens, first_row, rows_each, 0).astype(jnp.float32)
    partial_value = jnp.dot(part_kept.T, part_kept, preferred_element_type=jnp.float32)
    squares = jnp.sum(part_tokens * part_tokens)
    gramian, total_squares = lax.psum((partial_value, squares), ("section", "dp"))
    damping = 0.01 * total_squares / feature_count
    system = gramian + damping * jnp.eye(kept_count, dtype=jnp.float32)
    factor = jnp.linalg.cholesky(system)
    projected = jnp.dot(
        tokens,
        lax.all_gather(orig_weight, "dp", axis=0, tiled=True).T,
        preferred_element_type=jnp.float32,
    )
    partial_right = jnp.dot(kept_tokens.astype(jnp.float32).T, projected, precision=highest)
    right_own = lax.psum_scatter(partial_right, "dp", scatter_dimension=1, tiled=True)
    solution = jax.scipy.linalg.cho_solve((factor, True), right_own)
    corrected = (
        jnp.zeros((orig_weight.shape[0], feature_count), jnp.float32)
        .at[:, kept_index]
        .set(solution.T)
    )
    return corrected.astype(jnp.bfloat16)


def solution(mesh):
    in_specs = (P("dp", None), P(("section", "dp"), None), P())
    out_specs = P(("section", "dp"), None)
    return jax.shard_map(
        on_device, mesh=mesh, in_specs=in_specs, out_specs=out_specs, check_vma=False
    )
```

profile of v0, /device:TPU:1, one launch (start us, length us, event | category | flops | bytes accessed | tf_op | source)
XLA Modules:
  0.0 584.4 jit_solution(18266464242228412049)
XLA Ops:
  7.4 1.3 fusion.82
  8.7 0.7 fusion.81
  9.6 1.0 scatter_custom_fusion
  10.8 0.7 fusion.80
  11.7 3.3 copy.41
  15.0 2.7 gather_fusion
  17.9 2.0 fusion.19
  20.5 1.6 multiply_reduce_fusion
  22.1 107.7 %psum.15 = f32[]{:T(128)} all-reduce(f32[]{:T(128)} %multiply_reduce_fusion), channel_id=1, replica_groups=mesh['section'=16,'dp'=32] {'section','dp'}, use_global_device_ids=true, to_apply=%region_6.7 | all-reduce | flops 1 | bytes 8 | tf_op jit(solution)/shard_map/psum | solution.py:27
  130.4 180.2 %all-reduce.3.cloned.1.call-done = f32[768,768]{0,1:T(8,128)} async-done(((f32[768,768]{0,1:T(8,128)}), f32[768,768]{0,1:T(8,128)}) %all-reduce.3.cloned.1.call-update) | async-done | bytes 2359312 | tf_op jit(solution)/shard_map/psum | solution.py:27
  310.6 3.2 select_add_fusion
  313.8 3.7 copy.43
  317.5 2.0 fusion
  319.5 1.5 copy-done.1
  321.0 11.7 %cholesky.164 = f32[128,128]{1,0:T(8,128)S(1)} custom-call(f32[128,128]{1,0:T(8,128)S(1)} %cholesky.421), custom_call_target="Cholesky" | custom-call | tf_op jit(solution)/shard_map/jit(cholesky)/cholesky | solution.py:30
  332.8 9.8 %custom-call.50 = f32[1,128,128]{1,2,0:T(8,128)S(1)} custom-call(f32[1,128,128]{2,1,0:T(8,128)S(1)} %get-tuple-element.44), custom_call_target="InvertDiagBlocksLowerTriangular" | custom-call | tf_op jit(solution)/shard_map/jit(cholesky)/cholesky | solution.py:30
  342.6 1.4 fusion.9
  344.2 1.4 convolution_subtract_fusion
  345.6 11.7 %cholesky.187 = f32[128,128]{1,0:T(8,128)S(1)} custom-call(f32[128,128]{1,0:T(8,128)S(1)} %cholesky.425), custom_call_target="Cholesky" | custom-call | tf_op jit(solution)/shard_map/jit(cholesky)/cholesky | solution.py:30
  357.5 10.6 %custom-call.51 = f32[1,128,128]{1,2,0:T(8,128)} custom-call(f32[1,128,128]{2,1,0:T(8,128)S(1)} %get-tuple-element.42), custom_call_target="InvertDiagBlocksLowerTriangular" | custom-call | tf_op jit(solution)/shard_map/jit(cholesky)/cholesky | solution.py:30
  368.3 6.4 %fusion.92 = f32[256,1024]{1,0:T(8,128)S(1)} fusion(bf16[256,4096]{1,0:T(8,128)(2,1)} %param.3, bf16[1024,4096]{1,0:T(8,128)(2,1)} %all-gather.2.cloned.1.call-done), kind=kOutput, calls=%fused_computation.182 | convolution fusion | flops 2147483648 | bytes 11534336 | tf_op jit(solution)/shard_map/dot_general | solution.py:31
  374.7 3.3 fusion.93
  378.0 0.8 copy-done.2
  379.2 1.9 convolution_subtract_fusion.1
  381.2 11.7 %cholesky.352 = f32[128,128]{1,0:T(8,128)S(1)} custom-call(f32[128,128]{1,0:T(8,128)S(1)} %cholesky.430), custom_call_target="Cholesky" | custom-call | tf_op jit(solution)/shard_map/jit(cholesky)/cholesky | solution.py:30
  393.0 10.0 %custom-call.52 = f32[1,128,128]{1,2,0:T(8,128)S(1)} custom-call(f32[1,128,128]{2,1,0:T(8,128)S(1)} %get-tuple-element.40), custom_call_target="InvertDiagBlocksLowerTriangular" | custom-call | tf_op jit(solution)/shard_map/jit(cholesky)/cholesky | solution.py:30
  403.5 2.1 convolution_subtract_fusion.2
  405.6 11.7 %cholesky.371 = f32[128,128]{1,0:T(8,128)S(1)} custom-call(f32[128,128]{1,0:T(8,128)S(1)} %cholesky.435), custom_call_target="Cholesky" | custom-call | tf_op jit(solution)/shard_map/jit(cholesky)/cholesky | solution.py:30
  417.4 9.8 %custom-call.53 = f32[1,128,128]{1,2,0:T(8,128)S(1)} custom-call(f32[1,128,128]{2,1,0:T(8,128)S(1)} %get-tuple-element.38), custom_call_target="InvertDiagBlocksLowerTriangular" | custom-call | tf_op jit(solution)/shard_map/jit(cholesky)/cholesky | solution.py:30
  427.6 1.9 convolution_subtract_fusion.3
  429.5 12.1 %cholesky.390 = f32[128,128]{1,0:T(8,128)S(1)} custom-call(f32[128,128]{1,0:T(8,128)S(1)} %cholesky.440), custom_call_target="Cholesky" | custom-call | tf_op jit(solution)/shard_map/jit(cholesky)/cholesky | solution.py:30
  441.7 9.8 %custom-call.54 = f32[1,128,128]{1,2,0:T(8,128)S(1)} custom-call(f32[1,128,128]{2,1,0:T(8,128)S(1)} %get-tuple-element.36), custom_call_target="InvertDiagBlocksLowerTriangular" | custom-call | tf_op jit(solution)/shard_map/jit(cholesky)/cholesky | solution.py:30
  451.8 1.5 convolution_subtract_fusion.4
  453.4 11.7 %cholesky.408 = f32[128,128]{1,0:T(8,128)S(1)} custom-call(f32[128,128]{1,0:T(8,128)S(1)} %convolution_subtract_fusion.4), custom_call_target="Cholesky" | custom-call | tf_op jit(solution)/shard_map/jit(cholesky)/cholesky | solution.py:30
  465.2 0.6 compare_reduce_fusion.4
  467.0 0.6 compare_reduce_fusion.3
  468.3 0.6 compare_reduce_fusion.2
  469.6 0.6 compare_reduce_fusion.1
  470.9 0.6 compare_reduce_fusion
  472.2 1.6 select_select_fusion
  473.9 21.8 %while.1 = (s32[]{:T(128)}, f32[768,768]{0,1:T(8,128)}, s32[6,2]{0,1:T(2,128)S(1)}, f32[6,128,128]{2,1,0:T(8,128)}, s32[]{:T(128)}) while((s32[]{:T(128)}, f32[768,768]{0,1:T(8,128)}, s32[6,2]{0,1:T(2,128)S(1)}, f32[6,128,128]{2,1,0:T(8,128)}, s32[]{:T(128)}) %tuple.34), condition=%wide.while_cond, body=%wide.while_body.sunk | while | flops 2 | bytes 393329 | solution.py:38
  474.5 2.3 dynamic-slice.10
  478.2 2.3 dynamic-slice.10
  481.8 2.3 dynamic-slice.10
  484.2 0.6 bitcast_dynamic-update-slice_fusion.2
  485.4 2.3 dynamic-slice.10
  487.8 0.6 bitcast_dynamic-update-slice_fusion.2
  489.1 2.3 dynamic-slice.10
  491.5 0.6 bitcast_dynamic-update-slice_fusion.2
  492.7 2.2 dynamic-slice.10
  495.7 59.9 %custom-call.55 = f32[6,128,128]{1,2,0:T(8,128)S(1)} custom-call(f32[6,128,128]{2,1,0:T(8,128)} %get-tuple-element.12), custom_call_target="InvertDiagBlocksLowerTriangular" | custom-call | tf_op jit(solution)/shard_map/jit(_cho_solve)/triangular_solve | solution.py:38
  555.6 0.9 constant_dynamic-update-slice_fusion.4
  556.5 1.0 convolution_subtract_fusion.12
  557.7 1.1 convolution_subtract_fusion.11
  559.0 1.2 convolution_subtract_fusion.10
  560.4 1.2 convolution_subtract_fusion.9
  561.8 1.3 convolution_subtract_fusion.14
  563.4 1.1 convolution_subtract_fusion.8
  564.7 1.2 convolution_subtract_fusion.7
  566.1 1.3 convolution_subtract_fusion.6
  567.6 1.3 convolution_subtract_fusion.5
  569.2 1.4 convolution_subtract_fusion.13
  571.1 4.7 scatter_custom_fusion.1
  575.8 1.0 copy.57
  (98 shorter events, 12.7 us)
Async XLA Ops:
  7.4 303.2 %all-reduce.3.cloned.1.call-start = ((), (), s32[]{:S(2)}) async-start(), calls=%async_computation.1 | async-start | bytes 4718592 | tf_op jit(solution)/shard_map/psum | solution.py:27
  19.9 348.4 %all-gather.2.cloned.1.call-start = ((), (), s32[]{:S(2)}) async-start(), calls=%async_computation.2 | async-start | bytes 8650752 | tf_op jit(solution)/shard_map/all_gather | solution.py:33
  20.5 535.2 %reduce-scatter.2.cloned.1.call-start = ((), (), s32[]{:S(2)}) async-start(), calls=%async_computation.3 | async-start | bytes 3244032 | tf_op jit(solution)/shard_map/reduce_scatter | solution.py:37
  313.8 3.7 copy-start
  319.5 1.5 copy-start.1
  378.0 0.8 copy-start.2
Sparse Core Ops, SparseCore 0:
  20.0 290.5 all-reduce.2
Sparse Core Ops, SparseCore 1:
  22.5 78.7 all-gather.1
  378.1 146.9 reduce-scatter.1
where the time goes:
time: 589 us; the launch traced here: 584 us
  other arithmetic  197 us (33%)
  waiting for transfers between devices  181 us (31%)
  blocking collectives  108 us (18%)
  local copies, waits for them, and re-layouts  40.8 us (7%)
  matrix products  38.3 us (7%)
  between operations  20.1 us (3%)
    psum x1, waiting for transfers between devices, on_device(): lax.psum((partial_value, squares), ('section', 'dp'))  180 us
    another operation x22, other arithmetic, on_device(): factor = jnp.linalg.cholesky(system)  124 us
    psum x1, blocking collectives, on_device(): lax.psum((partial_value, squares), ('section', 'dp'))  108 us
    another operation x3, other arithmetic, on_device(): solution = jax.scipy.linalg.cho_solve((factor, True), right_own)  61.6 us
    another operation x31, local copies, waits for them, and re-layouts  21.8 us
    another operation x22, matrix products, on_device(): solution = jax.scipy.linalg.cho_solve((factor, True), right_own)  15 us
  transfers between devices with their start and end apart: 3, of which 1 were waited for; matrix products, arithmetic and copies ran while one was open for 39% of the time, Pallas kernels for 0%

commit v1 on v0

v1 whole, which is shorter than its diff:
```python
import functools

import jax
import jax.numpy as jnp
from jax import lax
from jax.experimental import pallas as pl
from jax.experimental.pallas import tpu as pltpu
from jax.sharding import PartitionSpec as P

HIGHEST = lax.Precision.HIGHEST
F32 = jnp.float32
BF16 = jnp.bfloat16
MESH = pl.DeviceIdType.MESH

KEEP_BLK = 12
KEEP = 768
TILE = 128
PANEL = 8
NBLOCK = KEEP // TILE
UNITS = NBLOCK * (NBLOCK + 1) // 2
WIDE = KEEP + TILE
CHUNK = 256


def _lower_block(t):
    row = jnp.int32(0)
    for i in range(1, NBLOCK):
        row = row + (t >= i * (i + 1) // 2).astype(jnp.int32)
    return row, t - row * (row + 1) // 2


def _half_swap(v):
    return pltpu.roll(v, 64, 1)


def prepare_kernel(flags, tokens, part, kept, kept_tokens, gram):
    section = lax.axis_index("section")

    def note(b, count):
        kept[count] = b
        return count + flags[b]

    lax.fori_loop(0, 64, note, jnp.int32(0))
    low = lax.broadcasted_iota(jnp.int32, (256, TILE), 1) < 64
    for i in range(NBLOCK):
        first, second = kept[2 * i], kept[2 * i + 1]
        a = tokens[:, pl.ds(pl.multiple_of((first // 2) * TILE, TILE), TILE)].astype(F32)
        b = tokens[:, pl.ds(pl.multiple_of((second // 2) * TILE, TILE), TILE)].astype(F32)
        a = jnp.where(first % 2 == 1, _half_swap(a), a)
        b = jnp.where(second % 2 == 0, _half_swap(b), b)
        kept_tokens[:, i * TILE : (i + 1) * TILE] = jnp.where(low, a, b).astype(BF16)
    chunk = tokens[:, pl.ds(pl.multiple_of(section * CHUNK, CHUNK), CHUNK)]
    over_tokens = (((0,), (0,)), ((), ()))
    part[:, 0:KEEP] = lax.dot_general(
        chunk, kept_tokens[...], over_tokens, preferred_element_type=F32
    )
    gram[...] = lax.dot_general(
        kept_tokens[...], kept_tokens[...], over_tokens, preferred_element_type=F32
    )
    for u in range(UNITS):
        unit = section * UNITS + u
        row, col = _lower_block(unit // 16)
        start = row * TILE + (unit % 16) * 8
        part[8 * u : 8 * u + 8, KEEP:WIDE] = gram[
            pl.ds(pl.multiple_of(start, 8), 8), pl.ds(pl.multiple_of(col * TILE, TILE), TILE)
        ]
    wide = chunk.astype(F32)
    squares = wide * wide
    squares = squares[:, :TILE] + squares[:, TILE:]
    total = squares[0:8]
    for g in range(1, 32):
        total = total + squares[8 * g : 8 * g + 8]
    part[8 * UNITS : 8 * UNITS + 8, KEEP:WIDE] = total
    part[8 * UNITS + 8 : 256, KEEP:WIDE] = jnp.zeros((256 - 8 * UNITS - 8, TILE), F32)


def tile_inverse(rows):
    lane = lax.broadcasted_iota(jnp.int32, (8, TILE), 1)
    sub = lax.broadcasted_iota(jnp.int32, (8, TILE), 0)
    panels = TILE // PANEL

    def over_lanes(v, c):
        return jnp.broadcast_to(v[:, c : c + 1], (8, TILE))

    def over_rows(v, q):
        return jnp.broadcast_to(v[q : q + 1, :], (8, TILE))

    for j in range(panels):
        base = j * PANEL
        columns = [over_lanes(rows[j], base + c) for c in range(PANEL)]
        inside = (lane >= base) & (lane < base + PANEL)
        r = jnp.where(inside, (lane - base == sub).astype(F32), rows[j])
        for q in range(PANEL):
            inv = 1.0 / over_rows(columns[q], q)
            pivot = sub == q
            m = jnp.where(pivot, 0.0, columns[q] * inv)
            scale = jnp.where(pivot, inv, 1.0)
            r = r * scale - m * over_rows(r, q)
            for c in range(q + 1, PANEL):
                columns[c] = columns[c] * scale - m * over_rows(columns[c], q)
        spread = [over_rows(r, c) for c in range(PANEL)]
        after = []
        for g in range(panels):
            if g == j:
                after.append(r)
                continue
            acc = jnp.where(inside, 0.0, rows[g])
            for c in range(PANEL):
                acc = acc - over_lanes(rows[g], base + c) * spread[c]
            after.append(acc)
        rows = after
    return rows


def eliminate(k, m, d):
    off = pl.multiple_of(k * TILE, TILE)
    rows = [m[pl.ds(pl.multiple_of(off + 8 * g, 8), 8), pl.ds(off, TILE)] for g in range(TILE // 8)]
    rows = tile_inverse(rows)
    for g in range(TILE // 8):
        d[8 * g : 8 * g + 8, :] = rows[g]
    col = lax.broadcasted_iota(jnp.int32, (TILE, KEEP), 1) - off
    row = lax.broadcasted_iota(jnp.int32, (TILE, KEEP), 0)
    inside = (col >= 0) & (col < TILE)
    r = jnp.where(inside, (col == row).astype(F32), m[pl.ds(off, TILE), :])
    r = jnp.dot(d[...], r, precision=HIGHEST, preferred_element_type=F32)
    for b in range(KEEP // 256):
        at = slice(256 * b, 256 * b + 256)
        c = m[at, pl.ds(off, TILE)]
        col = lax.broadcasted_iota(jnp.int32, (256, KEEP), 1) - off
        rest = jnp.where((col >= 0) & (col < TILE), 0.0, m[at, :])
        m[at, :] = rest - jnp.dot(c, r, precision=HIGHEST, preferred_element_type=F32)
    m[pl.ds(off, TILE), :] = r


def solve_kernel(
    part, weight, out,
    from_core, from_x, from_y, sums, shares, g_all, c_all, w_all, right, from_z, m, d, send, recv,
):
    section, dp = lax.axis_index("section"), lax.axis_index("dp")
    z, far = section // 2, section % 2
    x, y, core = dp // 8, (dp // 2) % 4, dp % 2

    def peer(axis, o):
        if axis == "z":
            return (lax.rem(z + o, 8) * 2 + far, dp)
        if axis == "far":
            return (z * 2 + 1 - far, dp)
        if axis == "x":
            return (section, lax.rem(x + o, 4) * 8 + y * 2 + core)
        if axis == "y":
            return (section, x * 8 + lax.rem(y + o, 4) * 2 + core)
        return (section, x * 8 + y * 2 + 1 - core)

    sizes = {"z": 8, "far": 2, "x": 4, "y": 4, "core": 2}
    barrier = pltpu.get_barrier_semaphore()
    greeted = 0
    for axis, n in sizes.items():
        for o in range(1, n):
            pl.semaphore_signal(barrier, inc=1, device_id=peer(axis, o), device_id_type=MESH)
            greeted += 1
    pl.semaphore_wait(barrier, greeted)

    slots = [0]

    def exchange(axis, source, target, landed):
        first = slots[0]
        n = sizes[axis]
        slots[0] += n - 1

        def copy(o, dst):
            at = first + o - 1
            return pltpu.make_async_remote_copy(
                src_ref=source(o), dst_ref=dst, send_sem=send.at[at], recv_sem=recv.at[at],
                device_id=peer(axis, o), device_id_type=MESH,
            )

        def start():
            for o in range(1, n):
                copy(o, target(o)).start()

        def wait():
            for o in range(1, n):
                copy(o, landed(o)).wait_send()
            for o in range(1, n):
                copy(o, landed(o)).wait_recv()

        return start, wait

    def at8(v, n=8):
        return pl.multiple_of(v, n)

    w_start, w_wait = exchange(
        "z",
        lambda o: weight.at[:, pl.ds(at8(lax.rem(z + o, 8) * 512, 512), 512)],
        lambda o: w_all.at[pl.ds(at8(z * 32, 32), 32), :],
        lambda o: w_all.at[pl.ds(at8(lax.rem(z + 8 - o, 8) * 32, 32), 32), :],
    )
    w_start()

    lanes = {"g": slice(KEEP, WIDE), "c": slice(0, KEEP)}
    stage = {}
    for name in ("g", "c"):
        cut = lanes[name]
        stage[name, "core"] = exchange(
            "core",
            lambda o, cut=cut: part.at[pl.ds(at8((1 - core) * 128, 128), 128), cut],
            lambda o, cut=cut: from_core.at[:, cut],
            lambda o, cut=cut: from_core.at[:, cut],
        )
        stage[name, "x"] = exchange(
            "x",
            lambda o, cut=cut: sums.at[pl.ds(at8(lax.rem(x + o, 4) * 32, 32), 32), cut],
            lambda o, cut=cut: from_x.at[o - 1, :, cut],
            lambda o, cut=cut: from_x.at[o - 1, :, cut],
        )
        stage[name, "y"] = exchange(
            "y",
            lambda o, cut=cut: shares.at[pl.ds(at8(lax.rem(y + o, 4) * 8), 8), cut],
            lambda o, cut=cut: from_y.at[o - 1, :, cut],
            lambda o, cut=cut: from_y.at[o - 1, :, cut],
        )

    def add_core(cut):
        sums[:, cut] = part[pl.ds(at8(core * 128, 128), 128), cut] + from_core[:, cut]

    def add_x(cut):
        own = sums[pl.ds(at8(x * 32, 32), 32), cut]
        shares[:, cut] = own + from_x[0, :, cut] + from_x[1, :, cut] + from_x[2, :, cut]

    def add_y(cut):
        own = shares[pl.ds(at8(y * 8), 8), cut]
        return own + from_y[0, :, cut] + from_y[1, :, cut] + from_y[2, :, cut]

    base = at8(core * 128 + x * 32 + y * 8)
    g_cut, c_cut = lanes["g"], lanes["c"]
    stage["g", "core"][0]()
    stage["c", "core"][0]()
    stage["g", "core"][1]()
    add_core(g_cut)
    stage["g", "x"][0]()
    stage["c", "core"][1]()
    add_core(c_cut)
    stage["c", "x"][0]()
    stage["g", "x"][1]()
    add_x(g_cut)
    stage["g", "y"][0]()
    stage["g", "y"][1]()
    g_all[z, far, pl.ds(base, 8), :] = add_y(g_cut)

    gz = exchange(
        "z",
        lambda o: g_all.at[z, far, pl.ds(base, 8), :],
        lambda o: g_all.at[z, far, pl.ds(base, 8), :],
        lambda o: g_all.at[lax.rem(z + 8 - o, 8), far, pl.ds(base, 8), :],
    )
    gfar = exchange(
        "far",
        lambda o: g_all.at[:, far, pl.ds(base, 8), :],
        lambda o: g_all.at[:, far, pl.ds(base, 8), :],
        lambda o: g_all.at[:, 1 - far, pl.ds(base, 8), :],
    )

    def row8(o):
        return at8(core * 128 + x * 32 + lax.rem(y + 4 - o, 4) * 8)

    def row32(o):
        return at8(core * 128 + lax.rem(x + 4 - o, 4) * 32, 32)

    gy = exchange(
        "y",
        lambda o: g_all.at[:, :, pl.ds(base, 8), :],
        lambda o: g_all.at[:, :, pl.ds(base, 8), :],
        lambda o: g_all.at[:, :, pl.ds(row8(o), 8), :],
    )
    gx = exchange(
        "x",
        lambda o: g_all.at[:, :, pl.ds(row32(0), 32), :],
        lambda o: g_all.at[:, :, pl.ds(row32(0), 32), :],
        lambda o: g_all.at[:, :, pl.ds(row32(o), 32), :],
    )
    gcore = exchange(
        "core",
        lambda o: g_all.at[:, :, pl.ds(at8(core * 128, 128), 128), :],
        lambda o: g_all.at[:, :, pl.ds(at8(core * 128, 128), 128), :],
        lambda o: g_all.at[:, :, pl.ds(at8((1 - core) * 128, 128), 128), :],
    )
    cfar = exchange(
        "far",
        lambda o: c_all.at[far, pl.ds(base, 8), :],
        lambda o: c_all.at[far, pl.ds(base, 8), :],
        lambda o: c_all.at[1 - far, pl.ds(base, 8), :],
    )
    cy = exchange(
        "y",
        lambda o: c_all.at[:, pl.ds(base, 8), :],
        lambda o: c_all.at[:, pl.ds(base, 8), :],
        lambda o: c_all.at[:, pl.ds(row8(o), 8), :],
    )
    cx = exchange(
        "x",
        lambda o: c_all.at[:, pl.ds(row32(0), 32), :],
        lambda o: c_all.at[:, pl.ds(row32(0), 32), :],
        lambda o: c_all.at[:, pl.ds(row32(o), 32), :],
    )
    ccore = exchange(
        "core",
        lambda o: c_all.at[:, pl.ds(at8(core * 128, 128), 128), :],
        lambda o: c_all.at[:, pl.ds(at8(core * 128, 128), 128), :],
        lambda o: c_all.at[:, pl.ds(at8((1 - core) * 128, 128), 128), :],
    )
    rz = exchange(
        "z",
        lambda o: right.at[pl.ds(at8(lax.rem(z + o, 8) * 32, 32), 32), :],
        lambda o: from_z.at[o - 1],
        lambda o: from_z.at[o - 1],
    )

    gz[0]()
    stage["c", "x"][1]()
    add_x(c_cut)
    stage["c", "y"][0]()
    gz[1]()
    gfar[0]()
    stage["c", "y"][1]()
    c_all[far, pl.ds(base, 8), :] = add_y(c_cut)
    cfar[0]()
    gfar[1]()
    gy[0]()
    cfar[1]()
    gy[1]()
    gx[0]()
    gx[1]()
    gcore[0]()
    cy[0]()
    w_all[pl.ds(at8(z * 32, 32), 32), :] = weight[:, pl.ds(at8(z * 512, 512), 512)]
    gcore[1]()

    total = jnp.zeros((8, TILE), F32)
    for s in range(16):
        total = total + g_all[s // 2, s % 2, 8 * UNITS : 8 * UNITS + 8, :]
    total = jnp.sum(jnp.sum(total, axis=0, keepdims=True), axis=1, keepdims=True)
    damping = 0.01 * total / 4096.0
    for t in range(UNITS):
        i = max(n for n in range(NBLOCK) if n * (n + 1) // 2 <= t)
        j = t - i * (i + 1) // 2
        for e in range(16):
            s, u = divmod(t * 16 + e, UNITS)
            m[i * TILE + 8 * e : i * TILE + 8 * e + 8, j * TILE : (j + 1) * TILE] = g_all[
                s // 2, s % 2, 8 * u : 8 * u + 8, :
            ]
        block = m[i * TILE : (i + 1) * TILE, j * TILE : (j + 1) * TILE]
        if i == j:
            eye = lax.broadcasted_iota(jnp.int32, (TILE, TILE), 0) == lax.broadcasted_iota(
                jnp.int32, (TILE, TILE), 1
            )
            m[i * TILE : (i + 1) * TILE, j * TILE : (j + 1) * TILE] = block + jnp.where(
                eye, damping, 0.0
            )
        else:
            m[j * TILE : (j + 1) * TILE, i * TILE : (i + 1) * TILE] = block.T

    def right_side():
        for b in range(2):
            c = c_all[b]
            high = c.astype(BF16)
            c = c - high.astype(F32)
            middle = c.astype(BF16)
            low = (c - middle.astype(F32)).astype(BF16)
            w = w_all[:, b * 256 : (b + 1) * 256]
            term = jnp.dot(w, high, preferred_element_type=F32)
            term += jnp.dot(w, middle, preferred_element_type=F32)
            term += jnp.dot(w, low, preferred_element_type=F32)
            if b == 0:
                right[...] = term
            else:
                right[...] += term

    @pl.loop(0, NBLOCK)
    def _(k):
        @pl.when(k == 0)
        def _():
            cy[1]()
            cx[0]()

        @pl.when(k == 1)
        def _():
            cx[1]()
            ccore[0]()

        @pl.when(k == 2)
        def _():
            ccore[1]()
            w_wait()
            right_side()
            rz[0]()

        eliminate(k, m, d)

    rz[1]()
    own = right[pl.ds(at8(z * 32, 32), 32), :]
    for o in range(7):
        own = own + from_z[o]
    out[...] = jnp.dot(own, m[...], precision=HIGHEST, preferred_element_type=F32)


def spread_kernel(flags, solved, out):
    low = lax.broadcasted_iota(jnp.int32, (32, TILE), 1) < 64
    rank = jnp.int32(0)
    for g in range(32):
        sides = []
        for side in range(2):
            flag = flags[2 * g + side]
            at = jnp.minimum(rank, KEEP_BLK - 1)
            v = solved[:, pl.ds(pl.multiple_of((at // 2) * TILE, TILE), TILE)]
            v = jnp.where(at % 2 == side, v, _half_swap(v))
            sides.append(jnp.where(flag == 1, v, 0.0))
            rank = rank + flag
        out[:, g * TILE : (g + 1) * TILE] = jnp.where(low, sides[0], sides[1]).astype(BF16)


def on_device(tokens, orig_weight, keep_flags):
    vmem = pl.BlockSpec(memory_space=pltpu.VMEM)
    smem = pl.BlockSpec(memory_space=pltpu.SMEM)
    part = pl.pallas_call(
        prepare_kernel,
        out_shape=jax.ShapeDtypeStruct((256, WIDE), F32),
        in_specs=[smem, vmem],
        out_specs=vmem,
        scratch_shapes=[
            pltpu.SMEM((16,), jnp.int32),
            pltpu.VMEM((256, KEEP), BF16),
            pltpu.VMEM((KEEP, KEEP), F32),
        ],
        name="prepare",
    )(keep_flags, tokens)
    solved = pl.pallas_call(
        solve_kernel,
        out_shape=jax.ShapeDtypeStruct((32, KEEP), F32),
        in_specs=[vmem, vmem],
        out_specs=vmem,
        scratch_shapes=[
            pltpu.VMEM((128, WIDE), F32),
            pltpu.VMEM((3, 32, WIDE), F32),
            pltpu.VMEM((3, 8, WIDE), F32),
            pltpu.VMEM((128, WIDE), F32),
            pltpu.VMEM((32, WIDE), F32),
            pltpu.VMEM((8, 2, 256, TILE), F32),
            pltpu.VMEM((2, 256, KEEP), F32),
            pltpu.VMEM((256, 512), BF16),
            pltpu.VMEM((256, KEEP), F32),
            pltpu.VMEM((7, 32, KEEP), F32),
            pltpu.VMEM((KEEP, KEEP), F32),
            pltpu.VMEM((TILE, TILE), F32),
            pltpu.SemaphoreType.DMA((64,)),
            pltpu.SemaphoreType.DMA((64,)),
        ],
        compiler_params=pltpu.CompilerParams(collective_id=0, has_side_effects=True),
        name="solve",
    )(part, orig_weight)
    return pl.pallas_call(
        spread_kernel,
        out_shape=jax.ShapeDtypeStruct((32, orig_weight.shape[1]), BF16),
        in_specs=[smem, vmem],
        out_specs=vmem,
        name="spread",
    )(keep_flags, solved)


def solution(mesh):
    in_specs = (P("dp", None), P(("section", "dp"), None), P())
    out_specs = P(("section", "dp"), None)
    return jax.shard_map(
        on_device, mesh=mesh, in_specs=in_specs, out_specs=out_specs, check_vma=False
    )
```

time: 589 us -> 117 us (0.20)
  other arithmetic: 197 us -> 0 us
  waiting for transfers between devices: 181 us -> 0 us
  Pallas kernels: 0 us -> 115 us
  blocking collectives: 108 us -> 0 us
  local copies, waits for them, and re-layouts: 40.8 us -> 0 us
  matrix products: 38.3 us -> 0 us
  between operations: 20.1 us -> 0.01 us
    another operation x28 -> x0, other arithmetic: 187 us -> none  [the longest x22 124 us: on_device(): factor = jnp.linalg.cholesky(system)]
    psum x1 -> x0, waiting for transfers between devices: 180 us -> none  [on_device(): lax.psum((partial_value, squares), ('section', 'dp'))]
    pallas_call x0 -> x3, Pallas kernels: none -> 115 us  [the longest x1 108 us: on_device(): pl.pallas_call(solve_kernel, out_shape=jax.ShapeDtypeStruct((32, KEEP), F...]
    psum x1 -> x0, blocking collectives: 108 us -> none  [on_device(): lax.psum((partial_value, squares), ('section', 'dp'))]
    another operation x32 -> x0, matrix products: 26.6 us -> none  [the longest x22 15 us: on_device(): solution = jax.scipy.linalg.cho_solve((factor, True), right_own)]
    another operation x54 -> x0, local copies, waits for them, and re-layouts: 23 us -> none
    dot_general x3 -> x0, matrix products: 11.7 us -> none  [the longest x1 6.38 us: on_device(): jnp.dot(tokens, lax.all_gather(orig_weight, 'dp', axis=0, tiled=True).T,...]
  transfers between devices with their start and end apart: 3 -> 0, of which waited for: 1 -> 0; matrix products, arithmetic and copies ran while one was open for 39% -> 0% of each run, Pallas kernels for 0% -> 0%
where the time goes in v1:
time: 117 us; the launch traced here: 115 us
  Pallas kernels  115 us (98%)
    pallas_call x1, Pallas kernels, on_device(): pl.pallas_call(solve_kernel, out_shape=jax.ShapeDtypeStruct((32, KEEP), F...  108 us
    pallas_call x1, Pallas kernels, on_device(): pl.pallas_call(prepare_kernel, out_shape=jax.ShapeDtypeStruct((256, WIDE)...  4.26 us

profile of v1, /device:TPU:1, one launch (start us, length us, event | category | flops | bytes accessed | tf_op | source)
XLA Modules:
  0.0 115.0 jit_solution(12153806897087171100)
XLA Ops:
  0.0 4.3 %prepare.1.part = f32[256,896]{1,0:T(8,128)} custom-call(s32[64]{0:T(128)} %flags.3, bf16[256,4096]{1,0:T(8,128)(2,1)} %tokens.1), custom_call_target="tpu_custom_call" | custom-call | tf_op jit(solution)/shard_map/prepare/pallas_call | solution.py:424
  4.3 108.5 %solve.1.solved = f32[32,768]{1,0:T(8,128)} custom-call(f32[256,896]{1,0:T(8,128)} %prepare.1.part, bf16[32,4096]{1,0:T(8,128)(2,1)} %weight.1), custom_call_target="tpu_custom_call" | custom-call | tf_op jit(solution)/shard_map/solve/pallas_call | solution.py:436
  112.8 2.3 %spread.1 = bf16[32,4096]{1,0:T(8,128)(2,1)} custom-call(s32[64]{0:T(128)} %flags.3, f32[32,768]{1,0:T(8,128)} %solve.1.solved), custom_call_target="tpu_custom_call" | custom-call | tf_op jit(solution)/shard_map/spread/pallas_call | solution.py:460

commit v2 on v1

--- a/solution.py
+++ b/solution.py
@@ -17,14 +17,15 @@
 TILE = 128
 PANEL = 8
 NBLOCK = KEEP // TILE
-UNITS = NBLOCK * (NBLOCK + 1) // 2
+FIRST = NBLOCK
+LATER = NBLOCK * (NBLOCK - 1) // 2
 WIDE = KEEP + TILE
 CHUNK = 256
 
 
 def _lower_block(t):
     row = jnp.int32(0)
-    for i in range(1, NBLOCK):
+    for i in range(1, NBLOCK - 1):
         row = row + (t >= i * (i + 1) // 2).astype(jnp.int32)
     return row, t - row * (row + 1) // 2
 
@@ -57,39 +58,51 @@
     gram[...] = lax.dot_general(
         kept_tokens[...], kept_tokens[...], over_tokens, preferred_element_type=F32
     )
-    for u in range(UNITS):
-        unit = section * UNITS + u
-        row, col = _lower_block(unit // 16)
+    part[:, KEEP:WIDE] = jnp.zeros((256, TILE), F32)
+
+    def put(at, unit, row, col):
         start = row * TILE + (unit % 16) * 8
-        part[8 * u : 8 * u + 8, KEEP:WIDE] = gram[
+        part[at : at + 8, KEEP:WIDE] = gram[
             pl.ds(pl.multiple_of(start, 8), 8), pl.ds(pl.multiple_of(col * TILE, TILE), TILE)
         ]
+
+    for u in range(FIRST):
+        unit = section * FIRST + u
+        put(32 * u, unit, unit // 16, 0)
+    for u in range(LATER):
+        unit = section * LATER + u
+        row, col = _lower_block(unit // 16)
+        put(32 * (u % 8) + 8 * (1 + u // 8), unit, row + 1, col + 1)
     wide = chunk.astype(F32)
     squares = wide * wide
     squares = squares[:, :TILE] + squares[:, TILE:]
     total = squares[0:8]
     for g in range(1, 32):
         total = total + squares[8 * g : 8 * g + 8]
-    part[8 * UNITS : 8 * UNITS + 8, KEEP:WIDE] = total
-    part[8 * UNITS + 8 : 256, KEEP:WIDE] = jnp.zeros((256 - 8 * UNITS - 8, TILE), F32)
-
-
-def tile_inverse(rows):
+    part[32 * FIRST : 32 * FIRST + 8, KEEP:WIDE] = total
+
+
+def tile_factors(rows, n, t, scratch):
     lane = lax.broadcasted_iota(jnp.int32, (8, TILE), 1)
     sub = lax.broadcasted_iota(jnp.int32, (8, TILE), 0)
     panels = TILE // PANEL
+    rows = list(rows)
 
     def over_lanes(v, c):
-        return jnp.broadcast_to(v[:, c : c + 1], (8, TILE))
+        column = jnp.sum(jnp.where(lane == c, v, 0.0), axis=1, keepdims=True)
+        return jnp.broadcast_to(column, (8, TILE))
 
     def over_rows(v, q):
         return jnp.broadcast_to(v[q : q + 1, :], (8, TILE))
 
     for j in range(panels):
         base = j * PANEL
-        columns = [over_lanes(rows[j], base + c) for c in range(PANEL)]
+        for c in range(PANEL):
+            scratch[8 * c : 8 * c + 8, :] = over_lanes(rows[j], base + c)
+        columns = [scratch[8 * c : 8 * c + 8, :] for c in range(PANEL)]
         inside = (lane >= base) & (lane < base + PANEL)
         r = jnp.where(inside, (lane - base == sub).astype(F32), rows[j])
+        n[base : base + 8, :] = jnp.where(lane < base + PANEL, r, 0.0)
         for q in range(PANEL):
             inv = 1.0 / over_rows(columns[q], q)
             pivot = sub == q
@@ -98,47 +111,75 @@
             r = r * scale - m * over_rows(r, q)
             for c in range(q + 1, PANEL):
                 columns[c] = columns[c] * scale - m * over_rows(columns[c], q)
+        t[base : base + 8, :] = jnp.where(lane < base + PANEL, r, 0.0)
         spread = [over_rows(r, c) for c in range(PANEL)]
-        after = []
-        for g in range(panels):
-            if g == j:
-                after.append(r)
-                continue
+        for g in range(j + 1, panels):
             acc = jnp.where(inside, 0.0, rows[g])
             for c in range(PANEL):
                 acc = acc - over_lanes(rows[g], base + c) * spread[c]
-            after.append(acc)
-        rows = after
-    return rows
-
-
-def eliminate(k, m, d):
+            rows[g] = acc
+
+
+def pieces(v):
+    high = v.astype(BF16)
+    v = v - high.astype(F32)
+    middle = v.astype(BF16)
+    return high, middle, (v - middle.astype(F32)).astype(BF16)
+
+
+def put_left(ref, rows, v):
+    high, middle, low = pieces(v)
+    for i, p in enumerate((high, high, middle, middle, high, low)):
+        ref[rows, i * TILE : (i + 1) * TILE] = p
+
+
+def put_right(ref, v):
+    high, middle, low = pieces(v)
+    for i, p in enumerate((high, middle, high, middle, low, high)):
+        ref[i * TILE : (i + 1) * TILE, :] = p
+
+
+def eliminate(k, m, lower, n, t, scratch, left, right, arrive):
     off = pl.multiple_of(k * TILE, TILE)
     rows = [m[pl.ds(pl.multiple_of(off + 8 * g, 8), 8), pl.ds(off, TILE)] for g in range(TILE // 8)]
-    rows = tile_inverse(rows)
-    for g in range(TILE // 8):
-        d[8 * g : 8 * g + 8, :] = rows[g]
+    tile_factors(rows, n, t, scratch)
+    arrive()
+    d = lax.dot_general(
+        n[...], t[...], (((0,), (0,)), ((), ())), precision=HIGHEST, preferred_element_type=F32
+    )
     col = lax.broadcasted_iota(jnp.int32, (TILE, KEEP), 1) - off
     row = lax.broadcasted_iota(jnp.int32, (TILE, KEEP), 0)
     inside = (col >= 0) & (col < TILE)
     r = jnp.where(inside, (col == row).astype(F32), m[pl.ds(off, TILE), :])
-    r = jnp.dot(d[...], r, precision=HIGHEST, preferred_element_type=F32)
-    for b in range(KEEP // 256):
-        at = slice(256 * b, 256 * b + 256)
-        c = m[at, pl.ds(off, TILE)]
-        col = lax.broadcasted_iota(jnp.int32, (256, KEEP), 1) - off
-        rest = jnp.where((col >= 0) & (col < TILE), 0.0, m[at, :])
-        m[at, :] = rest - jnp.dot(c, r, precision=HIGHEST, preferred_element_type=F32)
-    m[pl.ds(off, TILE), :] = r
+    lower[pl.ds(off, TILE), :] = jnp.where(col < TILE, r, 0.0)
+    put_left(left, slice(0, TILE), d)
+    put_right(right, r)
+    r = jnp.dot(left[0:TILE, :], right[...], preferred_element_type=F32)
+    m[pl.ds(off, TILE), :] = jnp.where(col < TILE, r, 0.0)
+    put_right(right, r)
+    for kk in range(NBLOCK - 1):
+
+        @pl.when(k == kk)
+        def _():
+            start = kk * TILE
+            stop = start + TILE
+            put_left(left, slice(stop, KEEP), m[stop:KEEP, start:stop])
+            p = jnp.dot(left[stop:KEEP, :], right[...], preferred_element_type=F32)
+            if kk:
+                m[stop:KEEP, 0:start] = m[stop:KEEP, 0:start] - p[:, 0:start]
+            m[stop:KEEP, start:stop] = -p[:, start:stop]
+            m[stop:KEEP, stop:KEEP] = m[stop:KEEP, stop:KEEP] - p[:, stop:KEEP]
 
 
 def solve_kernel(
     part, weight, out,
-    from_core, from_x, from_y, sums, shares, g_all, c_all, w_all, right, from_z, m, d, send, recv,
+    from_core, from_x, from_y, sums, shares, g_all, c_all, w_all, right, from_z,
+    m, lower, n_tile, t_tile, scratch, left_pieces, right_pieces, send, recv,
 ):
     section, dp = lax.axis_index("section"), lax.axis_index("dp")
     z, far = section // 2, section % 2
     x, y, core = dp // 8, (dp // 2) % 4, dp % 2
+    slot = lax.rem(y + 3, 4)
 
     def peer(axis, o):
         if axis == "z":
@@ -215,7 +256,7 @@
         )
         stage[name, "y"] = exchange(
             "y",
-            lambda o, cut=cut: shares.at[pl.ds(at8(lax.rem(y + o, 4) * 8), 8), cut],
+            lambda o, cut=cut: shares.at[pl.ds(at8(lax.rem(slot + o, 4) * 8), 8), cut],
             lambda o, cut=cut: from_y.at[o - 1, :, cut],
             lambda o, cut=cut: from_y.at[o - 1, :, cut],
         )
@@ -228,10 +269,10 @@
         shares[:, cut] = own + from_x[0, :, cut] + from_x[1, :, cut] + from_x[2, :, cut]
 
     def add_y(cut):
-        own = shares[pl.ds(at8(y * 8), 8), cut]
+        own = shares[pl.ds(at8(slot * 8), 8), cut]
         return own + from_y[0, :, cut] + from_y[1, :, cut] + from_y[2, :, cut]
 
-    base = at8(core * 128 + x * 32 + y * 8)
+    base = at8(core * 128 + x * 32 + slot * 8)
     g_cut, c_cut = lanes["g"], lanes["c"]
     stage["g", "core"][0]()
     stage["c", "core"][0]()
@@ -245,45 +286,82 @@
     add_x(g_cut)
     stage["g", "y"][0]()
     stage["g", "y"][1]()
-    g_all[z, far, pl.ds(base, 8), :] = add_y(g_cut)
+    own8 = pl.ds(at8(slot * 8), 8)
+    g_all[z, far, core, x, own8, :] = add_y(g_cut)
 
     gz = exchange(
         "z",
-        lambda o: g_all.at[z, far, pl.ds(base, 8), :],
-        lambda o: g_all.at[z, far, pl.ds(base, 8), :],
-        lambda o: g_all.at[lax.rem(z + 8 - o, 8), far, pl.ds(base, 8), :],
+        lambda o: g_all.at[z, far, core, x, own8, :],
+        lambda o: g_all.at[z, far, core, x, own8, :],
+        lambda o: g_all.at[lax.rem(z + 8 - o, 8), far, core, x, own8, :],
     )
     gfar = exchange(
         "far",
-        lambda o: g_all.at[:, far, pl.ds(base, 8), :],
-        lambda o: g_all.at[:, far, pl.ds(base, 8), :],
-        lambda o: g_all.at[:, 1 - far, pl.ds(base, 8), :],
+        lambda o: g_all.at[:, far, core, x, own8, :],
+        lambda o: g_all.at[:, far, core, x, own8, :],
+        lambda o: g_all.at[:, 1 - far, core, x, own8, :],
     )
 
     def row8(o):
-        return at8(core * 128 + x * 32 + lax.rem(y + 4 - o, 4) * 8)
+        return at8(core * 128 + x * 32 + lax.rem(slot + 4 - o, 4) * 8)
 
     def row32(o):
         return at8(core * 128 + lax.rem(x + 4 - o, 4) * 32, 32)
 
-    gy = exchange(
-        "y",
-        lambda o: g_all.at[:, :, pl.ds(base, 8), :],
-        lambda o: g_all.at[:, :, pl.ds(base, 8), :],
-        lambda o: g_all.at[:, :, pl.ds(row8(o), 8), :],
-    )
-    gx = exchange(
-        "x",
-        lambda o: g_all.at[:, :, pl.ds(row32(0), 32), :],
-        lambda o: g_all.at[:, :, pl.ds(row32(0), 32), :],
-        lambda o: g_all.at[:, :, pl.ds(row32(o), 32), :],
-    )
-    gcore = exchange(
-        "core",
-        lambda o: g_all.at[:, :, pl.ds(at8(core * 128, 128), 128), :],
-        lambda o: g_all.at[:, :, pl.ds(at8(core * 128, 128), 128), :],
-        lambda o: g_all.at[:, :, pl.ds(at8((1 - core) * 128, 128), 128), :],
-    )
+    y_slots = slots[0]
+    slots[0] += 3
+
+    def gy_copy(o):
+        rows = pl.ds(at8(lax.rem(slot + 4 - o, 4) * 8), 8)
+        return pltpu.make_async_remote_copy(
+            src_ref=g_all.at[:, :, core, x, own8, :],
+            dst_ref=g_all.at[:, :, core, x, rows, :],
+            send_sem=send.at[y_slots + o - 1], recv_sem=recv.at[y_slots + o - 1],
+            device_id=peer("y", o), device_id_type=MESH,
+        )
+
+    def gy_start():
+        @pl.when(slot < 3)
+        def _():
+            for o in range(1, 4):
+                pltpu.make_async_remote_copy(
+                    src_ref=g_all.at[:, :, core, x, own8, :],
+                    dst_ref=g_all.at[:, :, core, x, own8, :],
+                    send_sem=send.at[y_slots + o - 1], recv_sem=recv.at[y_slots + o - 1],
+                    device_id=peer("y", o), device_id_type=MESH,
+                ).start()
+
+    def gy_sent():
+        @pl.when(slot < 3)
+        def _():
+            for o in range(1, 4):
+                gy_copy(o).wait_send()
+
+    def gy_wait(first):
+        for o in range(1, 4):
+            source = lax.rem(slot + 4 - o, 4)
+
+            @pl.when((source == 0) if first else ((source == 1) | (source == 2)))
+            def _():
+                gy_copy(o).wait_recv()
+
+    def gather_rest(rows):
+        along_x = exchange(
+            "x",
+            lambda o: g_all.at[:, :, core, x, rows, :],
+            lambda o: g_all.at[:, :, core, x, rows, :],
+            lambda o: g_all.at[:, :, core, lax.rem(x + 4 - o, 4), rows, :],
+        )
+        along_core = exchange(
+            "core",
+            lambda o: g_all.at[:, :, core, :, rows, :],
+            lambda o: g_all.at[:, :, core, :, rows, :],
+            lambda o: g_all.at[:, :, 1 - core, :, rows, :],
+        )
+        return along_x, along_core
+
+    first_x, first_core = gather_rest(slice(0, 8))
+    later_x, later_core = gather_rest(slice(8, 24))
     cfar = exchange(
         "far",
         lambda o: c_all.at[far, pl.ds(base, 8), :],
@@ -325,39 +403,64 @@
     c_all[far, pl.ds(base, 8), :] = add_y(c_cut)
     cfar[0]()
     gfar[1]()
-    gy[0]()
+    gy_start()
     cfar[1]()
-    gy[1]()
-    gx[0]()
-    gx[1]()
-    gcore[0]()
     cy[0]()
+    gy_wait(True)
+    first_x[0]()
+    gy_wait(False)
+    later_x[0]()
+    cy[1]()
+    cx[0]()
     w_all[pl.ds(at8(z * 32, 32), 32), :] = weight[:, pl.ds(at8(z * 512, 512), 512)]
-    gcore[1]()
+    first_x[1]()
+    first_core[0]()
+    gy_sent()
+    first_core[1]()
 
     total = jnp.zeros((8, TILE), F32)
     for s in range(16):
-        total = total + g_all[s // 2, s % 2, 8 * UNITS : 8 * UNITS + 8, :]
+        total = total + g_all[s // 2, s % 2, FIRST // 4, FIRST % 4, 0:8, :]
     total = jnp.sum(jnp.sum(total, axis=0, keepdims=True), axis=1, keepdims=True)
     damping = 0.01 * total / 4096.0
-    for t in range(UNITS):
-        i = max(n for n in range(NBLOCK) if n * (n + 1) // 2 <= t)
-        j = t - i * (i + 1) // 2
+
+    def place(i, j, unit_at):
+        rows, cols = slice(i * TILE, (i + 1) * TILE), slice(j * TILE, (j + 1) * TILE)
         for e in range(16):
-            s, u = divmod(t * 16 + e, UNITS)
-            m[i * TILE + 8 * e : i * TILE + 8 * e + 8, j * TILE : (j + 1) * TILE] = g_all[
-                s // 2, s % 2, 8 * u : 8 * u + 8, :
-            ]
-        block = m[i * TILE : (i + 1) * TILE, j * TILE : (j + 1) * TILE]
+            m[i * TILE + 8 * e : i * TILE + 8 * e + 8, cols] = unit_at(e)
+        block = m[rows, cols]
         if i == j:
             eye = lax.broadcasted_iota(jnp.int32, (TILE, TILE), 0) == lax.broadcasted_iota(
                 jnp.int32, (TILE, TILE), 1
             )
-            m[i * TILE : (i + 1) * TILE, j * TILE : (j + 1) * TILE] = block + jnp.where(
-                eye, damping, 0.0
-            )
+            m[rows, cols] = block + jnp.where(eye, damping, 0.0)
         else:
-            m[j * TILE : (j + 1) * TILE, i * TILE : (i + 1) * TILE] = block.T
+            m[cols, rows] = block.T
+
+    for i in range(NBLOCK):
+
+        def first_unit(e, i=i):
+            s, u = divmod(i * 16 + e, FIRST)
+            return g_all[s // 2, s % 2, u // 4, u % 4, 0:8, :]
+
+        place(i, 0, first_unit)
+
+    def later_blocks():
+        later_x[1]()
+        later_core[0]()
+        later_core[1]()
+        block = 0
+        for i in range(1, NBLOCK):
+            for j in range(1, i + 1):
+
+                def later_unit(e, block=block):
+                    s, u = divmod(block * 16 + e, LATER)
+                    q = u % 8
+                    at = 8 * (1 + u // 8)
+                    return g_all[s // 2, s % 2, q // 4, q % 4, at : at + 8, :]
+
+                place(i, j, later_unit)
+                block += 1
 
     def right_side():
         for b in range(2):
@@ -377,11 +480,6 @@
 
     @pl.loop(0, NBLOCK)
     def _(k):
-        @pl.when(k == 0)
-        def _():
-            cy[1]()
-            cx[0]()
-
         @pl.when(k == 1)
         def _():
             cx[1]()
@@ -394,12 +492,20 @@
             right_side()
             rz[0]()
 
-        eliminate(k, m, d)
+        def arrive():
+            pl.when(k == 0)(later_blocks)
+
+        eliminate(
+            k, m, lower, n_tile, t_tile, scratch, left_pieces, right_pieces, arrive
+        )
 
     rz[1]()
     own = right[pl.ds(at8(z * 32, 32), 32), :]
     for o in range(7):
         own = own + from_z[o]
+    own = lax.dot_general(
+        own, lower[...], (((1,), (1,)), ((), ())), precision=HIGHEST, preferred_element_type=F32
+    )
     out[...] = jnp.dot(own, m[...], precision=HIGHEST, preferred_element_type=F32)
 
 
@@ -444,13 +550,18 @@
             pltpu.VMEM((3, 8, WIDE), F32),
             pltpu.VMEM((128, WIDE), F32),
             pltpu.VMEM((32, WIDE), F32),
-            pltpu.VMEM((8, 2, 256, TILE), F32),
+            pltpu.VMEM((8, 2, 2, 4, 32, TILE), F32),
             pltpu.VMEM((2, 256, KEEP), F32),
             pltpu.VMEM((256, 512), BF16),
             pltpu.VMEM((256, KEEP), F32),
             pltpu.VMEM((7, 32, KEEP), F32),
             pltpu.VMEM((KEEP, KEEP), F32),
+            pltpu.VMEM((KEEP, KEEP), F32),
             pltpu.VMEM((TILE, TILE), F32),
+            pltpu.VMEM((TILE, TILE), F32),
+            pltpu.VMEM((8 * PANEL, TILE), F32),
+            pltpu.VMEM((KEEP, KEEP), BF16),
+            pltpu.VMEM((KEEP, KEEP), BF16),
             pltpu.SemaphoreType.DMA((64,)),
             pltpu.SemaphoreType.DMA((64,)),
         ],

time: 117 us -> 90.7 us (0.78)
  Pallas kernels: 115 us -> 89.4 us
    pallas_call x1, Pallas kernels: 108 us -> 82.9 us  [on_device(): pl.pallas_call(solve_kernel, out_shape=jax.ShapeDtypeStruct((32, KEEP), F...]
where the time goes in v2:
time: 90.7 us; the launch traced here: 89.4 us
  Pallas kernels  89.4 us (99%)
    pallas_call x1, Pallas kernels, on_device(): pl.pallas_call(solve_kernel, out_shape=jax.ShapeDtypeStruct((32, KEEP), F...  82.9 us
    pallas_call x1, Pallas kernels, on_device(): pl.pallas_call(prepare_kernel, out_shape=jax.ShapeDtypeStruct((256, WIDE)...  4.2 us
    pallas_call x1, Pallas kernels, on_device(): pl.pallas_call(spread_kernel, out_shape=jax.ShapeDtypeStruct((32, orig_we...  2.27 us

profile of v2, /device:TPU:1, one launch (start us, length us, event | category | flops | bytes accessed | tf_op | source)
XLA Modules:
  0.0 89.4 jit_solution(3425179193347600978)
XLA Ops:
  0.0 4.2 %prepare.1.part = f32[256,896]{1,0:T(8,128)} custom-call(s32[64]{0:T(128)} %flags.3, bf16[256,4096]{1,0:T(8,128)(2,1)} %tokens.1), custom_call_target="tpu_custom_call" | custom-call | tf_op jit(solution)/shard_map/prepare/pallas_call | solution.py:530
  4.2 82.9 %solve.1.solved = f32[32,768]{1,0:T(8,128)} custom-call(f32[256,896]{1,0:T(8,128)} %prepare.1.part, bf16[32,4096]{1,0:T(8,128)(2,1)} %weight.1), custom_call_target="tpu_custom_call" | custom-call | tf_op jit(solution)/shard_map/solve/pallas_call | solution.py:542
  87.1 2.3 %spread.1 = bf16[32,4096]{1,0:T(8,128)(2,1)} custom-call(s32[64]{0:T(128)} %flags.3, f32[32,768]{1,0:T(8,128)} %solve.1.solved), custom_call_target="tpu_custom_call" | custom-call | tf_op jit(solution)/shard_map/spread/pallas_call | solution.py:571

commit v3 on v2

--- a/solution.py
+++ b/solution.py
@@ -184,19 +184,20 @@
     def peer(axis, o):
         if axis == "z":
             return (lax.rem(z + o, 8) * 2 + far, dp)
-        if axis == "far":
-            return (z * 2 + 1 - far, dp)
+        if axis == "ring":
+            at = lax.rem(far * 4 + y + o, 8)
+            return (z * 2 + at // 4, x * 8 + lax.rem(at, 4) * 2 + core)
         if axis == "x":
             return (section, lax.rem(x + o, 4) * 8 + y * 2 + core)
         if axis == "y":
             return (section, x * 8 + lax.rem(y + o, 4) * 2 + core)
         return (section, x * 8 + y * 2 + 1 - core)
 
-    sizes = {"z": 8, "far": 2, "x": 4, "y": 4, "core": 2}
+    sizes = {"z": 8, "ring": 8, "x": 4, "y": 4, "core": 2}
     barrier = pltpu.get_barrier_semaphore()
     greeted = 0
-    for axis, n in sizes.items():
-        for o in range(1, n):
+    for axis in ("z", "ring", "x", "core"):
+        for o in range(1, sizes[axis]):
             pl.semaphore_signal(barrier, inc=1, device_id=peer(axis, o), device_id_type=MESH)
             greeted += 1
     pl.semaphore_wait(barrier, greeted)
@@ -238,9 +239,10 @@
     )
     w_start()
 
-    lanes = {"g": slice(KEEP, WIDE), "c": slice(0, KEEP)}
+    halves = (0, 1)
+    lanes = {"g": slice(KEEP, WIDE), 0: slice(0, KEEP // 2), 1: slice(KEEP // 2, KEEP)}
     stage = {}
-    for name in ("g", "c"):
+    for name in ("g", 0, 1):
         cut = lanes[name]
         stage[name, "core"] = exchange(
             "core",
@@ -273,18 +275,29 @@
         return own + from_y[0, :, cut] + from_y[1, :, cut] + from_y[2, :, cut]
 
     base = at8(core * 128 + x * 32 + slot * 8)
-    g_cut, c_cut = lanes["g"], lanes["c"]
+    g_cut = lanes["g"]
     stage["g", "core"][0]()
-    stage["c", "core"][0]()
+    for h in halves:
+        stage[h, "core"][0]()
+
+    def c_to_x(h):
+        stage[h, "core"][1]()
+        add_core(lanes[h])
+        stage[h, "x"][0]()
+
+    def c_to_y(h):
+        stage[h, "x"][1]()
+        add_x(lanes[h])
+        stage[h, "y"][0]()
+
     stage["g", "core"][1]()
     add_core(g_cut)
     stage["g", "x"][0]()
-    stage["c", "core"][1]()
-    add_core(c_cut)
-    stage["c", "x"][0]()
+    c_to_x(0)
     stage["g", "x"][1]()
     add_x(g_cut)
     stage["g", "y"][0]()
+    c_to_x(1)
     stage["g", "y"][1]()
     own8 = pl.ds(at8(slot * 8), 8)
     g_all[z, far, core, x, own8, :] = add_y(g_cut)
@@ -295,55 +308,43 @@
         lambda o: g_all.at[z, far, core, x, own8, :],
         lambda o: g_all.at[lax.rem(z + 8 - o, 8), far, core, x, own8, :],
     )
-    gfar = exchange(
-        "far",
-        lambda o: g_all.at[:, far, core, x, own8, :],
-        lambda o: g_all.at[:, far, core, x, own8, :],
-        lambda o: g_all.at[:, 1 - far, core, x, own8, :],
-    )
-
-    def row8(o):
-        return at8(core * 128 + x * 32 + lax.rem(slot + 4 - o, 4) * 8)
+    def ring_source(o):
+        at = lax.rem(far * 4 + y + 8 - o, 8)
+        return at // 4, lax.rem(at + 3, 4)
 
     def row32(o):
         return at8(core * 128 + lax.rem(x + 4 - o, 4) * 32, 32)
 
-    y_slots = slots[0]
-    slots[0] += 3
-
-    def gy_copy(o):
-        rows = pl.ds(at8(lax.rem(slot + 4 - o, 4) * 8), 8)
+    ring_slots = slots[0]
+    slots[0] += 7
+
+    def ring_copy(o, dst):
+        at = ring_slots + o - 1
         return pltpu.make_async_remote_copy(
-            src_ref=g_all.at[:, :, core, x, own8, :],
-            dst_ref=g_all.at[:, :, core, x, rows, :],
-            send_sem=send.at[y_slots + o - 1], recv_sem=recv.at[y_slots + o - 1],
-            device_id=peer("y", o), device_id_type=MESH,
-        )
-
-    def gy_start():
+            src_ref=g_all.at[:, far, core, x, own8, :], dst_ref=dst, send_sem=send.at[at],
+            recv_sem=recv.at[at], device_id=peer("ring", o), device_id_type=MESH,
+        )
+
+    def ring_start():
         @pl.when(slot < 3)
         def _():
-            for o in range(1, 4):
-                pltpu.make_async_remote_copy(
-                    src_ref=g_all.at[:, :, core, x, own8, :],
-                    dst_ref=g_all.at[:, :, core, x, own8, :],
-                    send_sem=send.at[y_slots + o - 1], recv_sem=recv.at[y_slots + o - 1],
-                    device_id=peer("y", o), device_id_type=MESH,
-                ).start()
-
-    def gy_sent():
+            for o in range(1, 8):
+                ring_copy(o, g_all.at[:, far, core, x, own8, :]).start()
+
+    def ring_sent():
         @pl.when(slot < 3)
         def _():
-            for o in range(1, 4):
-                gy_copy(o).wait_send()
-
-    def gy_wait(first):
-        for o in range(1, 4):
-            source = lax.rem(slot + 4 - o, 4)
+            for o in range(1, 8):
+                ring_copy(o, g_all.at[:, far, core, x, own8, :]).wait_send()
+
+    def ring_wait(first):
+        for o in range(1, 8):
+            source_far, source = ring_source(o)
 
             @pl.when((source == 0) if first else ((source == 1) | (source == 2)))
             def _():
-                gy_copy(o).wait_recv()
+                rows = pl.ds(at8(source * 8), 8)
+                ring_copy(o, g_all.at[:, source_far, core, x, rows, :]).wait_recv()
 
     def gather_rest(rows):
         along_x = exchange(
@@ -362,60 +363,70 @@
 
     first_x, first_core = gather_rest(slice(0, 8))
     later_x, later_core = gather_rest(slice(8, 24))
-    cfar = exchange(
-        "far",
-        lambda o: c_all.at[far, pl.ds(base, 8), :],
-        lambda o: c_all.at[far, pl.ds(base, 8), :],
-        lambda o: c_all.at[1 - far, pl.ds(base, 8), :],
-    )
-    cy = exchange(
-        "y",
-        lambda o: c_all.at[:, pl.ds(base, 8), :],
-        lambda o: c_all.at[:, pl.ds(base, 8), :],
-        lambda o: c_all.at[:, pl.ds(row8(o), 8), :],
-    )
-    cx = exchange(
-        "x",
-        lambda o: c_all.at[:, pl.ds(row32(0), 32), :],
-        lambda o: c_all.at[:, pl.ds(row32(0), 32), :],
-        lambda o: c_all.at[:, pl.ds(row32(o), 32), :],
-    )
-    ccore = exchange(
-        "core",
-        lambda o: c_all.at[:, pl.ds(at8(core * 128, 128), 128), :],
-        lambda o: c_all.at[:, pl.ds(at8(core * 128, 128), 128), :],
-        lambda o: c_all.at[:, pl.ds(at8((1 - core) * 128, 128), 128), :],
-    )
-    rz = exchange(
-        "z",
-        lambda o: right.at[pl.ds(at8(lax.rem(z + o, 8) * 32, 32), 32), :],
-        lambda o: from_z.at[o - 1],
-        lambda o: from_z.at[o - 1],
-    )
+    c_ring, cx, ccore, rz = {}, {}, {}, {}
+    for h in halves:
+        half = lanes[h]
+
+        def c_landed(o, half=half):
+            source_far, source = ring_source(o)
+            rows = pl.ds(at8(core * 128 + x * 32 + source * 8), 8)
+            return c_all.at[source_far, rows, half]
+
+        c_ring[h] = exchange(
+            "ring",
+            lambda o, half=half: c_all.at[far, pl.ds(base, 8), half],
+            lambda o, half=half: c_all.at[far, pl.ds(base, 8), half],
+            c_landed,
+        )
+        cx[h] = exchange(
+            "x",
+            lambda o, half=half: c_all.at[:, pl.ds(row32(0), 32), half],
+            lambda o, half=half: c_all.at[:, pl.ds(row32(0), 32), half],
+            lambda o, half=half: c_all.at[:, pl.ds(row32(o), 32), half],
+        )
+        ccore[h] = exchange(
+            "core",
+            lambda o, half=half: c_all.at[:, pl.ds(at8(core * 128, 128), 128), half],
+            lambda o, half=half: c_all.at[:, pl.ds(at8(core * 128, 128), 128), half],
+            lambda o, half=half: c_all.at[:, pl.ds(at8((1 - core) * 128, 128), 128), half],
+        )
+        rz[h] = exchange(
+            "z",
+            lambda o, half=half: right.at[pl.ds(at8(lax.rem(z + o, 8) * 32, 32), 32), half],
+            lambda o, half=half: from_z.at[o - 1, :, half],
+            lambda o, half=half: from_z.at[o - 1, :, half],
+        )
+
+    def c_to_ring(h):
+        stage[h, "y"][1]()
+        c_all[far, pl.ds(base, 8), lanes[h]] = add_y(lanes[h])
+        c_ring[h][0]()
+
+    def c_gather_x(h):
+        c_ring[h][1]()
+        cx[h][0]()
+
+    def c_gather_core(h):
+        cx[h][1]()
+        ccore[h][0]()
 
     gz[0]()
-    stage["c", "x"][1]()
-    add_x(c_cut)
-    stage["c", "y"][0]()
+    c_to_y(0)
+    c_to_y(1)
     gz[1]()
-    gfar[0]()
-    stage["c", "y"][1]()
-    c_all[far, pl.ds(base, 8), :] = add_y(c_cut)
-    cfar[0]()
-    gfar[1]()
-    gy_start()
-    cfar[1]()
-    cy[0]()
-    gy_wait(True)
+    ring_start()
+    c_to_ring(0)
+    c_to_ring(1)
+    ring_wait(True)
     first_x[0]()
-    gy_wait(False)
+    ring_wait(False)
     later_x[0]()
-    cy[1]()
-    cx[0]()
-    w_all[pl.ds(at8(z * 32, 32), 32), :] = weight[:, pl.ds(at8(z * 512, 512), 512)]
+    c_gather_x(0)
     first_x[1]()
     first_core[0]()
-    gy_sent()
+    c_gather_x(1)
+    w_all[pl.ds(at8(z * 32, 32), 32), :] = weight[:, pl.ds(at8(z * 512, 512), 512)]
+    ring_sent()
     first_core[1]()
 
     total = jnp.zeros((8, TILE), F32)
@@ -462,44 +473,45 @@
                 place(i, j, later_unit)
                 block += 1
 
-    def right_side():
+    def right_side(h):
+        ccore[h][1]()
         for b in range(2):
-            c = c_all[b]
-            high = c.astype(BF16)
-            c = c - high.astype(F32)
-            middle = c.astype(BF16)
-            low = (c - middle.astype(F32)).astype(BF16)
+            high, middle, low = pieces(c_all[b, :, lanes[h]])
             w = w_all[:, b * 256 : (b + 1) * 256]
             term = jnp.dot(w, high, preferred_element_type=F32)
             term += jnp.dot(w, middle, preferred_element_type=F32)
             term += jnp.dot(w, low, preferred_element_type=F32)
             if b == 0:
-                right[...] = term
+                right[:, lanes[h]] = term
             else:
-                right[...] += term
+                right[:, lanes[h]] += term
+        rz[h][0]()
 
     @pl.loop(0, NBLOCK)
     def _(k):
         @pl.when(k == 1)
         def _():
-            cx[1]()
-            ccore[0]()
+            c_gather_core(1)
 
         @pl.when(k == 2)
         def _():
-            ccore[1]()
-            w_wait()
-            right_side()
-            rz[0]()
+            right_side(1)
 
         def arrive():
-            pl.when(k == 0)(later_blocks)
-
-        eliminate(
-            k, m, lower, n_tile, t_tile, scratch, left_pieces, right_pieces, arrive
-        )
-
-    rz[1]()
+            @pl.when(k == 0)
+            def _():
+                later_blocks()
+                c_gather_core(0)
+
+            @pl.when(k == 1)
+            def _():
+                w_wait()
+                right_side(0)
+
+        eliminate(k, m, lower, n_tile, t_tile, scratch, left_pieces, right_pieces, arrive)
+
+    rz[0][1]()
+    rz[1][1]()
     own = right[pl.ds(at8(z * 32, 32), 32), :]
     for o in range(7):
         own = own + from_z[o]
@@ -562,8 +574,8 @@
             pltpu.VMEM((8 * PANEL, TILE), F32),
             pltpu.VMEM((KEEP, KEEP), BF16),
             pltpu.VMEM((KEEP, KEEP), BF16),
-            pltpu.SemaphoreType.DMA((64,)),
-            pltpu.SemaphoreType.DMA((64,)),
+            pltpu.SemaphoreType.DMA((96,)),
+            pltpu.SemaphoreType.DMA((96,)),
         ],
         compiler_params=pltpu.CompilerParams(collective_id=0, has_side_effects=True),
         name="solve",

time: 90.7 us -> 88.6 us (0.977)
  Pallas kernels: 89.4 us -> 87.8 us
    pallas_call x1, Pallas kernels: 82.9 us -> 81.3 us  [on_device(): pl.pallas_call(solve_kernel, out_shape=jax.ShapeDtypeStruct((32, KEEP), F...]
where the time goes in v3:
time: 88.6 us; the launch traced here: 87.8 us
  Pallas kernels  87.8 us (99%)
    pallas_call x1, Pallas kernels, on_device(): pl.pallas_call(solve_kernel, out_shape=jax.ShapeDtypeStruct((32, KEEP), F...  81.3 us
    pallas_call x1, Pallas kernels, on_device(): pl.pallas_call(prepare_kernel, out_shape=jax.ShapeDtypeStruct((256, WIDE)...  4.2 us
    pallas_call x1, Pallas kernels, on_device(): pl.pallas_call(spread_kernel, out_shape=jax.ShapeDtypeStruct((32, orig_we...  2.27 us

profile of v3, /device:TPU:1, one launch (start us, length us, event | category | flops | bytes accessed | tf_op | source)
XLA Modules:
  0.0 87.8 jit_solution(5301993896139605132)
XLA Ops:
  0.0 4.2 %prepare.1.part = f32[256,896]{1,0:T(8,128)} custom-call(s32[64]{0:T(128)} %flags.3, bf16[256,4096]{1,0:T(8,128)(2,1)} %tokens.1), custom_call_target="tpu_custom_call" | custom-call | tf_op jit(solution)/shard_map/prepare/pallas_call | solution.py:542
  4.2 81.3 %solve.1.solved = f32[32,768]{1,0:T(8,128)} custom-call(f32[256,896]{1,0:T(8,128)} %prepare.1.part, bf16[32,4096]{1,0:T(8,128)(2,1)} %weight.1), custom_call_target="tpu_custom_call" | custom-call | tf_op jit(solution)/shard_map/solve/pallas_call | solution.py:554
  85.6 2.3 %spread.1 = bf16[32,4096]{1,0:T(8,128)(2,1)} custom-call(s32[64]{0:T(128)} %flags.3, f32[32,768]{1,0:T(8,128)} %solve.1.solved), custom_call_target="tpu_custom_call" | custom-call | tf_op jit(solution)/shard_map/spread/pallas_call | solution.py:583

commit v4 on v3

--- a/solution.py
+++ b/solution.py
@@ -95,11 +95,16 @@
     def over_rows(v, q):
         return jnp.broadcast_to(v[q : q + 1, :], (8, TILE))
 
+    for c in range(PANEL):
+        scratch[8 * c : 8 * c + 8, :] = over_lanes(rows[0], c)
+    columns = [scratch[8 * c : 8 * c + 8, :] for c in range(PANEL)]
     for j in range(panels):
         base = j * PANEL
-        for c in range(PANEL):
-            scratch[8 * c : 8 * c + 8, :] = over_lanes(rows[j], base + c)
-        columns = [scratch[8 * c : 8 * c + 8, :] for c in range(PANEL)]
+        more = j + 1 < panels
+        if more:
+            ahead = [over_lanes(rows[j], base + PANEL + c) for c in range(PANEL)]
+            below = [over_lanes(rows[j + 1], base + c) for c in range(PANEL)]
+            coming = [over_lanes(rows[j + 1], base + PANEL + c) for c in range(PANEL)]
         inside = (lane >= base) & (lane < base + PANEL)
         r = jnp.where(inside, (lane - base == sub).astype(F32), rows[j])
         n[base : base + 8, :] = jnp.where(lane < base + PANEL, r, 0.0)
@@ -111,12 +116,23 @@
             r = r * scale - m * over_rows(r, q)
             for c in range(q + 1, PANEL):
                 columns[c] = columns[c] * scale - m * over_rows(columns[c], q)
+            if more:
+                for c in range(PANEL):
+                    ahead[c] = ahead[c] * scale - m * over_rows(ahead[c], q)
         t[base : base + 8, :] = jnp.where(lane < base + PANEL, r, 0.0)
+        if more:
+            columns = []
+            for c in range(PANEL):
+                terms = [below[q] * over_rows(ahead[c], q) for q in range(PANEL)]
+                while len(terms) > 1:
+                    terms = [a + b for a, b in zip(terms[::2], terms[1::2])]
+                columns.append(coming[c] - terms[0])
         spread = [over_rows(r, c) for c in range(PANEL)]
         for g in range(j + 1, panels):
             acc = jnp.where(inside, 0.0, rows[g])
             for c in range(PANEL):
-                acc = acc - over_lanes(rows[g], base + c) * spread[c]
+                factor = below[c] if g == j + 1 else over_lanes(rows[g], base + c)
+                acc = acc - factor * spread[c]
             rows[g] = acc
 
 
@@ -239,10 +255,12 @@
     )
     w_start()
 
-    halves = (0, 1)
-    lanes = {"g": slice(KEEP, WIDE), 0: slice(0, KEEP // 2), 1: slice(KEEP // 2, KEEP)}
+    thirds = (0, 1, 2)
+    lanes = {"g": slice(KEEP, WIDE)}
+    for h in thirds:
+        lanes[h] = slice(h * KEEP // 3, (h + 1) * KEEP // 3)
     stage = {}
-    for name in ("g", 0, 1):
+    for name in ("g", *thirds):
         cut = lanes[name]
         stage[name, "core"] = exchange(
             "core",
@@ -277,7 +295,7 @@
     base = at8(core * 128 + x * 32 + slot * 8)
     g_cut = lanes["g"]
     stage["g", "core"][0]()
-    for h in halves:
+    for h in thirds:
         stage[h, "core"][0]()
 
     def c_to_x(h):
@@ -298,6 +316,7 @@
     add_x(g_cut)
     stage["g", "y"][0]()
     c_to_x(1)
+    c_to_x(2)
     stage["g", "y"][1]()
     own8 = pl.ds(at8(slot * 8), 8)
     g_all[z, far, core, x, own8, :] = add_y(g_cut)
@@ -364,37 +383,37 @@
     first_x, first_core = gather_rest(slice(0, 8))
     later_x, later_core = gather_rest(slice(8, 24))
     c_ring, cx, ccore, rz = {}, {}, {}, {}
-    for h in halves:
-        half = lanes[h]
-
-        def c_landed(o, half=half):
+    for h in thirds:
+        third = lanes[h]
+
+        def c_landed(o, third=third):
             source_far, source = ring_source(o)
             rows = pl.ds(at8(core * 128 + x * 32 + source * 8), 8)
-            return c_all.at[source_far, rows, half]
+            return c_all.at[source_far, rows, third]
 
         c_ring[h] = exchange(
             "ring",
-            lambda o, half=half: c_all.at[far, pl.ds(base, 8), half],
-            lambda o, half=half: c_all.at[far, pl.ds(base, 8), half],
+            lambda o, third=third: c_all.at[far, pl.ds(base, 8), third],
+            lambda o, third=third: c_all.at[far, pl.ds(base, 8), third],
             c_landed,
         )
         cx[h] = exchange(
             "x",
-            lambda o, half=half: c_all.at[:, pl.ds(row32(0), 32), half],
-            lambda o, half=half: c_all.at[:, pl.ds(row32(0), 32), half],
-            lambda o, half=half: c_all.at[:, pl.ds(row32(o), 32), half],
+            lambda o, third=third: c_all.at[:, pl.ds(row32(0), 32), third],
+            lambda o, third=third: c_all.at[:, pl.ds(row32(0), 32), third],
+            lambda o, third=third: c_all.at[:, pl.ds(row32(o), 32), third],
         )
         ccore[h] = exchange(
             "core",
-            lambda o, half=half: c_all.at[:, pl.ds(at8(core * 128, 128), 128), half],
-            lambda o, half=half: c_all.at[:, pl.ds(at8(core * 128, 128), 128), half],
-            lambda o, half=half: c_all.at[:, pl.ds(at8((1 - core) * 128, 128), 128), half],
+            lambda o, third=third: c_all.at[:, pl.ds(at8(core * 128, 128), 128), third],
+            lambda o, third=third: c_all.at[:, pl.ds(at8(core * 128, 128), 128), third],
+            lambda o, third=third: c_all.at[:, pl.ds(at8((1 - core) * 128, 128), 128), third],
         )
         rz[h] = exchange(
             "z",
-            lambda o, half=half: right.at[pl.ds(at8(lax.rem(z + o, 8) * 32, 32), 32), half],
-            lambda o, half=half: from_z.at[o - 1, :, half],
-            lambda o, half=half: from_z.at[o - 1, :, half],
+            lambda o, third=third: right.at[pl.ds(at8(lax.rem(z + o, 8) * 32, 32), 32), third],
+            lambda o, third=third: from_z.at[o - 1, :, third],
+            lambda o, third=third: from_z.at[o - 1, :, third],
         )
 
     def c_to_ring(h):
@@ -411,20 +430,21 @@
         ccore[h][0]()
 
     gz[0]()
-    c_to_y(0)
-    c_to_y(1)
+    for h in thirds:
+        c_to_y(h)
     gz[1]()
     ring_start()
-    c_to_ring(0)
-    c_to_ring(1)
+    for h in thirds:
+        c_to_ring(h)
     ring_wait(True)
     first_x[0]()
+    c_gather_x(0)
     ring_wait(False)
     later_x[0]()
-    c_gather_x(0)
     first_x[1]()
     first_core[0]()
     c_gather_x(1)
+    c_gather_x(2)
     w_all[pl.ds(at8(z * 32, 32), 32), :] = weight[:, pl.ds(at8(z * 512, 512), 512)]
     ring_sent()
     first_core[1]()
@@ -457,8 +477,10 @@
         place(i, 0, first_unit)
 
     def later_blocks():
+        c_gather_core(0)
         later_x[1]()
         later_core[0]()
+        c_gather_core(1)
         later_core[1]()
         block = 0
         for i in range(1, NBLOCK):
@@ -491,27 +513,27 @@
     def _(k):
         @pl.when(k == 1)
         def _():
-            c_gather_core(1)
+            w_wait()
+            right_side(0)
+            c_gather_core(2)
 
         @pl.when(k == 2)
         def _():
-            right_side(1)
+            right_side(2)
 
         def arrive():
             @pl.when(k == 0)
             def _():
                 later_blocks()
-                c_gather_core(0)
 
             @pl.when(k == 1)
             def _():
-                w_wait()
-                right_side(0)
+                right_side(1)
 
         eliminate(k, m, lower, n_tile, t_tile, scratch, left_pieces, right_pieces, arrive)
 
-    rz[0][1]()
-    rz[1][1]()
+    for h in thirds:
+        rz[h][1]()
     own = right[pl.ds(at8(z * 32, 32), 32), :]
     for o in range(7):
         own = own + from_z[o]
@@ -574,8 +596,8 @@
             pltpu.VMEM((8 * PANEL, TILE), F32),
             pltpu.VMEM((KEEP, KEEP), BF16),
             pltpu.VMEM((KEEP, KEEP), BF16),
-            pltpu.SemaphoreType.DMA((96,)),
-            pltpu.SemaphoreType.DMA((96,)),
+            pltpu.SemaphoreType.DMA((128,)),
+            pltpu.SemaphoreType.DMA((128,)),
         ],
         compiler_params=pltpu.CompilerParams(collective_id=0, has_side_effects=True),
         name="solve",

time: 88.6 us -> 87.3 us (0.985)
  no operation moved by 1% of the time
where the time goes in v4:
time: 87.3 us; the launch traced here: 87.1 us
  Pallas kernels  87.1 us (100%)
    pallas_call x1, Pallas kernels, on_device(): pl.pallas_call(solve_kernel, out_shape=jax.ShapeDtypeStruct((32, KEEP), F...  80.6 us
    pallas_call x1, Pallas kernels, on_device(): pl.pallas_call(prepare_kernel, out_shape=jax.ShapeDtypeStruct((256, WIDE)...  4.2 us
    pallas_call x1, Pallas kernels, on_device(): pl.pallas_call(spread_kernel, out_shape=jax.ShapeDtypeStruct((32, orig_we...  2.27 us

profile of v4, /device:TPU:1, one launch (start us, length us, event | category | flops | bytes accessed | tf_op | source)
XLA Modules:
  0.0 87.1 jit_solution(13502794571155032660)
XLA Ops:
  0.0 4.2 %prepare.1.part = f32[256,896]{1,0:T(8,128)} custom-call(s32[64]{0:T(128)} %flags.3, bf16[256,4096]{1,0:T(8,128)(2,1)} %tokens.1), custom_call_target="tpu_custom_call" | custom-call | tf_op jit(solution)/shard_map/prepare/pallas_call | solution.py:564
  4.2 80.6 %solve.1.solved = f32[32,768]{1,0:T(8,128)} custom-call(f32[256,896]{1,0:T(8,128)} %prepare.1.part, bf16[32,4096]{1,0:T(8,128)(2,1)} %weight.1), custom_call_target="tpu_custom_call" | custom-call | tf_op jit(solution)/shard_map/solve/pallas_call | solution.py:576
  84.8 2.3 %spread.1 = bf16[32,4096]{1,0:T(8,128)(2,1)} custom-call(s32[64]{0:T(128)} %flags.3, f32[32,768]{1,0:T(8,128)} %solve.1.solved), custom_call_target="tpu_custom_call" | custom-call | tf_op jit(solution)/shard_map/spread/pallas_call | solution.py:605

commit v5 on v4

--- a/solution.py
+++ b/solution.py
@@ -37,11 +37,10 @@
 def prepare_kernel(flags, tokens, part, kept, kept_tokens, gram):
     section = lax.axis_index("section")
 
-    def note(b, count):
+    count = jnp.int32(0)
+    for b in range(64):
         kept[count] = b
-        return count + flags[b]
-
-    lax.fori_loop(0, 64, note, jnp.int32(0))
+        count = count + flags[b]
     low = lax.broadcasted_iota(jnp.int32, (256, TILE), 1) < 64
     for i in range(NBLOCK):
         first, second = kept[2 * i], kept[2 * i + 1]
@@ -190,7 +189,7 @@
 def solve_kernel(
     part, weight, out,
     from_core, from_x, from_y, sums, shares, g_all, c_all, w_all, right, from_z,
-    m, lower, n_tile, t_tile, scratch, left_pieces, right_pieces, send, recv,
+    m, lower, n_tile, t_tile, scratch, left_pieces, right_pieces, lower_pieces, m_pieces, send, recv,
 ):
     section, dp = lax.axis_index("section"), lax.axis_index("dp")
     z, far = section // 2, section % 2
@@ -532,15 +531,32 @@
 
         eliminate(k, m, lower, n_tile, t_tile, scratch, left_pieces, right_pieces, arrive)
 
+    for b in range(NBLOCK):
+        rows = slice(b * TILE, (b + 1) * TILE)
+        for i, p in enumerate(pieces(lower[rows, :])):
+            lower_pieces[i, rows, :] = p
+        for i, p in enumerate(pieces(m[rows, :])):
+            m_pieces[i, rows, :] = p
+
+    def times(v, factor, contract):
+        stack = jnp.concatenate(pieces(v), axis=0)
+        total = None
+        for i in range(3):
+            p = lax.dot_general(
+                stack[0 : 32 * (3 - i), :], factor[i], (((1,), (contract,)), ((), ())),
+                preferred_element_type=F32,
+            )
+            for at in range(3 - i):
+                part_of = p[32 * at : 32 * at + 32, :]
+                total = part_of if total is None else total + part_of
+        return total
+
     for h in thirds:
         rz[h][1]()
     own = right[pl.ds(at8(z * 32, 32), 32), :]
     for o in range(7):
         own = own + from_z[o]
-    own = lax.dot_general(
-        own, lower[...], (((1,), (1,)), ((), ())), precision=HIGHEST, preferred_element_type=F32
-    )
-    out[...] = jnp.dot(own, m[...], precision=HIGHEST, preferred_element_type=F32)
+    out[...] = times(times(own, lower_pieces, 1), m_pieces, 0)
 
 
 def spread_kernel(flags, solved, out):
@@ -596,6 +612,8 @@
             pltpu.VMEM((8 * PANEL, TILE), F32),
             pltpu.VMEM((KEEP, KEEP), BF16),
             pltpu.VMEM((KEEP, KEEP), BF16),
+            pltpu.VMEM((3, KEEP, KEEP), BF16),
+            pltpu.VMEM((3, KEEP, KEEP), BF16),
             pltpu.SemaphoreType.DMA((128,)),
             pltpu.SemaphoreType.DMA((128,)),
         ],

time: 87.3 us -> 86.7 us (level)
  no operation moved by 1% of the time
where the time goes in v5:
time: 86.7 us; the launch traced here: 86.5 us
  Pallas kernels  86.5 us (100%)
    pallas_call x1, Pallas kernels, on_device(): pl.pallas_call(solve_kernel, out_shape=jax.ShapeDtypeStruct((32, KEEP), F...  80.5 us
    pallas_call x1, Pallas kernels, on_device(): pl.pallas_call(prepare_kernel, out_shape=jax.ShapeDtypeStruct((256, WIDE)...  3.69 us
    pallas_call x1, Pallas kernels, on_device(): pl.pallas_call(spread_kernel, out_shape=jax.ShapeDtypeStruct((32, orig_we...  2.27 us

profile of v5, /device:TPU:1, one launch (start us, length us, event | category | flops | bytes accessed | tf_op | source)
XLA Modules:
  0.0 86.5 jit_solution(6135923359241107413)
XLA Ops:
  0.0 3.7 %prepare.1.part = f32[256,896]{1,0:T(8,128)} custom-call(s32[64]{0:T(128)} %flags.3, bf16[256,4096]{1,0:T(8,128)(2,1)} %tokens.1), custom_call_target="tpu_custom_call" | custom-call | tf_op jit(solution)/shard_map/prepare/pallas_call | solution.py:580
  3.7 80.5 %solve.1.solved = f32[32,768]{1,0:T(8,128)} custom-call(f32[256,896]{1,0:T(8,128)} %prepare.1.part, bf16[32,4096]{1,0:T(8,128)(2,1)} %weight.1), custom_call_target="tpu_custom_call" | custom-call | tf_op jit(solution)/shard_map/solve/pallas_call | solution.py:592
  84.2 2.3 %spread.1 = bf16[32,4096]{1,0:T(8,128)(2,1)} custom-call(s32[64]{0:T(128)} %flags.3, f32[32,768]{1,0:T(8,128)} %solve.1.solved), custom_call_target="tpu_custom_call" | custom-call | tf_op jit(solution)/shard_map/spread/pallas_call | solution.py:623

commit v6 on v5

--- a/solution.py
+++ b/solution.py
@@ -218,6 +218,7 @@
     pl.semaphore_wait(barrier, greeted)
 
     slots = [0]
+    all_sent = []
 
     def exchange(axis, source, target, landed):
         first = slots[0]
@@ -237,10 +238,13 @@
 
         def wait():
             for o in range(1, n):
-                copy(o, landed(o)).wait_send()
+                copy(o, landed(o)).wait_recv()
+
+        def sent():
             for o in range(1, n):
-                copy(o, landed(o)).wait_recv()
-
+                copy(o, target(o)).wait_send()
+
+        all_sent.append(sent)
         return start, wait
 
     def at8(v, n=8):
@@ -445,7 +449,7 @@
     c_gather_x(1)
     c_gather_x(2)
     w_all[pl.ds(at8(z * 32, 32), 32), :] = weight[:, pl.ds(at8(z * 512, 512), 512)]
-    ring_sent()
+    all_sent.append(ring_sent)
     first_core[1]()
 
     total = jnp.zeros((8, TILE), F32)
@@ -557,6 +561,8 @@
     for o in range(7):
         own = own + from_z[o]
     out[...] = times(times(own, lower_pieces, 1), m_pieces, 0)
+    for sent in all_sent:
+        sent()
 
 
 def spread_kernel(flags, solved, out):

time: 86.7 us -> 86.8 us (level)
  no operation moved by 1% of the time
where the time goes in v6:
time: 86.8 us; the launch traced here: 86.6 us
  Pallas kernels  86.6 us (100%)
    pallas_call x1, Pallas kernels, on_device(): pl.pallas_call(solve_kernel, out_shape=jax.ShapeDtypeStruct((32, KEEP), F...  80.7 us
    pallas_call x1, Pallas kernels, on_device(): pl.pallas_call(prepare_kernel, out_shape=jax.ShapeDtypeStruct((256, WIDE)...  3.68 us
    pallas_call x1, Pallas kernels, on_device(): pl.pallas_call(spread_kernel, out_shape=jax.ShapeDtypeStruct((32, orig_we...  2.27 us

profile of v6, /device:TPU:1, one launch (start us, length us, event | category | flops | bytes accessed | tf_op | source)
XLA Modules:
  0.0 86.6 jit_solution(16838144464184129340)
XLA Ops:
  0.0 3.7 %prepare.1.part = f32[256,896]{1,0:T(8,128)} custom-call(s32[64]{0:T(128)} %flags.3, bf16[256,4096]{1,0:T(8,128)(2,1)} %tokens.1), custom_call_target="tpu_custom_call" | custom-call | tf_op jit(solution)/shard_map/prepare/pallas_call | solution.py:586
  3.7 80.7 %solve.1.solved = f32[32,768]{1,0:T(8,128)} custom-call(f32[256,896]{1,0:T(8,128)} %prepare.1.part, bf16[32,4096]{1,0:T(8,128)(2,1)} %weight.1), custom_call_target="tpu_custom_call" | custom-call | tf_op jit(solution)/shard_map/solve/pallas_call | solution.py:598
  84.4 2.3 %spread.1 = bf16[32,4096]{1,0:T(8,128)(2,1)} custom-call(s32[64]{0:T(128)} %flags.3, f32[32,768]{1,0:T(8,128)} %solve.1.solved), custom_call_target="tpu_custom_call" | custom-call | tf_op jit(solution)/shard_map/spread/pallas_call | solution.py:629
